TPU v7x, 512 devices: a whole 4x8x8 slice. The times are simulated.
512 devices in a mesh: segment: 4 (over x), graph: 128 (over y, z, core).
Axes of the slice: x: 4, y: 8, z: 8, core: 2. Of those that a mesh axis runs over, the one named last changes fastest.
Arguments:
- features: bfloat16 [65536, 1024], P('graph'), may hold values from -6 to 6
- weights: bfloat16 [8, 1024, 1024], P(None, 'graph'), may hold values from -0.75 to 0.75
- history: bfloat16 [8, 8192, 1024], P(None, 'graph'), may hold values from 0 to 1.1953125
- own_adj: bfloat16 [4, 16384, 128], P(None, 'graph'), may hold values from 0 to 0.00390625
- side_adj: bfloat16 [4, 4, 2048, 128], P(None, None, 'graph'), may hold values from 0 to 0.012451172
- hist_adj: bfloat16 [4, 8192, 128], P(None, 'graph'), may hold values from 0 to 0.009338379
- send_ids: int32 [4, 4, 2048], P(None, None, 'graph'), may hold values from 0 to 127, as said below
- hist_ids: int32 [4, 8192], P(None, 'graph'), may hold values from 0 to 63
Outputs:
- layer_out: bfloat16 [8, 65536, 1024], P('segment', 'graph')
Inputs may be any that keep to these rules, and one draw needn't show every extreme that they name: `send_ids`: each list of 16 row numbers for one batch, one partition and one direction has distinct entries.
All inputs are finite; a program needn't handle non-finite values.
Results may differ from a plain program's by a relative error of at most 0.0032.
Values may be sent and summed in bfloat16 or wider, within the bound.
No kernel may reach another device: no remote copies, remote signals or barrier semaphores. Data moves between devices by JAX's collectives and lax.ppermute only.
A program may use at most 64 MiB of HBM per device.

v0:
```python
import jax
import jax.numpy as jnp
from jax import lax
from jax.sharding import PartitionSpec as P

ALPHA = 0.1
LAMBDA = 1.5
BF = jnp.bfloat16
F32 = jnp.float32


def dot(a, b):
    return jnp.dot(a, b, preferred_element_type=F32)


def dot_t(a, b):
    return lax.dot_general(a, b, (((0,), (0,)), ((), ())), preferred_element_type=F32)


def one_hot(ids, width):
    return (ids[:, None] == lax.broadcasted_iota(jnp.int32, (ids.shape[0], width), 1)).astype(BF)


def shards(features, weights, history, own_adj, side_adj, hist_adj, send_ids, hist_ids):
    segment_pos = lax.axis_index("segment")
    segment_count = lax.axis_size("segment")
    graph_count = lax.axis_size("graph")
    core = lax.axis_index("graph") % 2
    chip_odd = lax.axis_index("graph") // 2 % 2
    layers, _, width = weights.shape
    rows = own_adj.shape[2]
    edge = send_ids.shape[2]
    kept = layers // segment_count
    resident = lax.all_gather(weights, "graph", axis=1, tiled=True)

    def partner(value):
        return lax.ppermute(value, "graph", [(p, p ^ 1) for p in range(graph_count)])

    def exchange(value, first):
        pairs = []
        for p in range(first, graph_count - first - 2, 4):
            for c in range(2):
                pairs += [(p + c, p + c + 2), (p + c + 2, p + c)]
        return lax.ppermute(value, "graph", pairs)

    def pick_batch(value):
        return lax.dynamic_index_in_dim(value, segment_pos, 0, keepdims=False)

    def by_part(mine, theirs):
        return (jnp.where(core == 0, mine, theirs), jnp.where(core == 0, theirs, mine))

    initial = lax.dynamic_slice_in_dim(features, segment_pos * rows, rows, 0)
    own = pick_batch(own_adj)
    side = pick_batch(side_adj).reshape(4 * edge, rows)
    hist = pick_batch(hist_adj)
    sids = pick_batch(send_ids).reshape(-1)
    hids = pick_batch(hist_ids)
    tables = jnp.concatenate([own, side, hist], axis=0)
    ids = jnp.concatenate([sids, hids])
    i0, i1 = by_part(ids, partner(ids))
    t0, t1 = by_part(tables, partner(tables))
    x0, x1 = by_part(initial, partner(initial))
    looked = jax.vmap(lambda t: dot(one_hot(hids, t.shape[0]), t).astype(BF))(history)
    g0, g1 = by_part(looked, partner(looked))

    def split(t, i):
        own = t[:rows]
        side = [t[rows + k * edge : rows + (k + 1) * edge] for k in range(4)]
        hist = t[rows + 4 * edge :]
        send = [one_hot(i[k * edge : (k + 1) * edge], rows) for k in range(4)]
        return (own, side, hist, send)

    own0, side0, hist0, send0 = split(t0, i0)
    own1, side1, hist1, send1 = split(t1, i1)
    q10 = dot_t(side1[0], send0[0]).astype(BF)
    q01 = dot_t(side0[1], send1[1]).astype(BF)
    near = jnp.concatenate(
        [jnp.concatenate([own0, q01], axis=1), jnp.concatenate([q10, own1], axis=1)], axis=0
    )
    zs = jnp.zeros_like(side0[0])
    from_before = jnp.concatenate(
        [
            jnp.concatenate([side0[0], side0[2], zs], axis=0),
            jnp.concatenate([zs, zs, side1[2]], axis=0),
        ],
        axis=1,
    )
    from_after = jnp.concatenate(
        [
            jnp.concatenate([side0[3], zs, zs], axis=0),
            jnp.concatenate([zs, side1[1], side1[3]], axis=0),
        ],
        axis=1,
    )
    to_after = jnp.concatenate(
        [
            jnp.concatenate([zs, send1[0]], axis=1),
            jnp.concatenate([send0[2], zs], axis=1),
            jnp.concatenate([zs, send1[2]], axis=1),
        ],
        axis=0,
    )
    to_before = jnp.concatenate(
        [
            jnp.concatenate([send0[3], zs], axis=1),
            jnp.concatenate([send0[1], zs], axis=1),
            jnp.concatenate([zs, send1[3]], axis=1),
        ],
        axis=0,
    )
    far_a = jnp.where(chip_odd == 0, from_after, from_before)
    far_b = jnp.where(chip_odd == 0, from_before, from_after)
    pick_a = jnp.where(chip_odd == 0, to_after, to_before)
    pick_b = jnp.where(chip_odd == 0, to_before, to_after)
    zh = jnp.zeros_like(hist0)
    hist_t = jnp.concatenate(
        [jnp.concatenate([hist0, zh], axis=1), jnp.concatenate([zh, hist1], axis=1)], axis=0
    )
    looked = jnp.concatenate([g0, g1], axis=1)
    start = jnp.concatenate([x0, x1], axis=0)
    current = start
    own_rows = []
    for layer in range(layers):
        strength = jnp.log(jnp.float32(LAMBDA / (layer + 1.0)) + 1.0)
        got_a = exchange(dot(pick_a, current).astype(BF), 0)
        got_b = exchange(dot(pick_b, current).astype(BF), 2)
        local = dot(near, current) + dot_t(hist_t, looked[layer])
        total = local + dot_t(far_a, got_a) + dot_t(far_b, got_b)
        support = (1.0 - ALPHA) * total + ALPHA * start.astype(F32)
        mixing = dot(support.astype(BF), resident[layer])
        current = jax.nn.relu((1.0 - strength) * support + strength * mixing).astype(BF)
        own_rows.append(lax.dynamic_slice_in_dim(current, core * rows, rows, 0))
    whole = jnp.stack(own_rows).reshape(segment_count, kept, rows, width)
    exchanged = lax.all_to_all(whole, "segment", 0, 0)
    return exchanged.transpose(1, 0, 2, 3).reshape(kept, segment_count * rows, width)


def solution(mesh):
    in_specs = (
        P("graph", None),
        P(None, "graph", None),
        P(None, "graph", None),
        P(None, "graph", None),
        P(None, None, "graph", None),
        P(None, "graph", None),
        P(None, None, "graph"),
        P(None, "graph"),
    )
    out_specs = P("segment", "graph", None)
    return jax.shard_map(shards, mesh=mesh, in_specs=in_specs, out_specs=out_specs, check_vma=False)
```

profile of v0, /device:TPU:32, one launch (start us, length us, event | category | flops | bytes accessed | tf_op | source)
XLA Modules:
  0.0 252.8 jit_solution(157648303293373457)
XLA Ops:
  8.8 1.9 collective-permute-start.1
  11.7 2.4 collective-permute-start.2
  16.8 1.9 collective-permute-start
  19.2 2.4 collective-permute-start.3
  23.7 1.1 broadcast_select_fusion.3
  25.1 10.8 %collective-permute-start.5 = (bf16[48,1024]{1,0:T(8,128)(2,1)S(1)}, bf16[48,1024]{1,0:T(8,128)(2,1)S(1)}, u32[]{:S(2)}, u32[]{:S(2)}) collective-permute-start(bf16[48,1024]{1,0:T(8,128)(2,1)S(1)} %convolution_convert_fusion.15), channel_id=1, source_target_pairs={{2,4},{4,2},{3,5},{5,3},{6,8},{8,6},{7,9},{9,7},{10,12},{12,10},{1... | collective-permute-start | bytes 294920 | tf_op jit(solution)/shard_map/ppermute | solution.py:44
  36.1 1.9 collective-permute-start.4
  39.4 3.6 %collective-permute-done.4 = bf16[48,1024]{1,0:T(8,128)(2,1)S(1)} collective-permute-done((bf16[48,1024]{1,0:T(8,128)(2,1)S(1)}, bf16[48,1024]{1,0:T(8,128)(2,1)S(1)}, u32[]{:S(2)}, u32[]{:S(2)}) %collective-permute-start.4) | collective-permute-done | bytes 98336 | tf_op jit(solution)/shard_map/ppermute | solution.py:44
  43.3 1.4 broadcast_select_fusion
  45.0 1.4 fusion.19
  46.5 68.9 %all-gather.2.cloned.1.call-done = bf16[8,1024,1024]{2,1,0:T(8,128)(2,1)} async-done(((bf16[8,8,1024]{2,1,0:T(8,128)(2,1)}), bf16[8,1024,1024]{2,1,0:T(8,128)(2,1)}) %all-gather.2.cloned.1.call-update) | async-done | bytes 16777232 | tf_op jit(solution)/shard_map/all_gather | solution.py:34
  115.3 3.1 %maximum_convert_fusion.6 = bf16[256,1024]{1,0:T(8,128)(2,1)S(1)} fusion(f32[256,1024]{1,0:T(8,128)} %fusion.19, bf16[8,1024,1024]{2,1,0:T(8,128)(2,1)} %all-gather.2.cloned.1.call-done), kind=kOutput, calls=%fused_computation.103 | convolution fusion | flops 538443776 | bytes 4718592 | tf_op jit(solution)/shard_map/dot_general | solution.py:13
  119.2 4.4 %collective-permute-start.7 = (bf16[48,1024]{1,0:T(8,128)(2,1)S(1)}, bf16[48,1024]{1,0:T(8,128)(2,1)S(1)}, u32[]{:S(2)}, u32[]{:S(2)}) collective-permute-start(bf16[48,1024]{1,0:T(8,128)(2,1)S(1)} %convolution_convert_fusion.13), channel_id=1, source_target_pairs={{2,4},{4,2},{3,5},{5,3},{6,8},{8,6},{7,9},{9,7},{10,12},{12,10},{1... | collective-permute-start | bytes 294920 | tf_op jit(solution)/shard_map/ppermute | solution.py:44
  123.9 1.9 collective-permute-start.6
  125.8 3.5 %collective-permute-done.7 = bf16[48,1024]{1,0:T(8,128)(2,1)S(1)} collective-permute-done((bf16[48,1024]{1,0:T(8,128)(2,1)S(1)}, bf16[48,1024]{1,0:T(8,128)(2,1)S(1)}, u32[]{:S(2)}, u32[]{:S(2)}) %collective-permute-start.7) | collective-permute-done | bytes 98336 | tf_op jit(solution)/shard_map/ppermute | solution.py:44
  130.8 2.4 maximum_convert_fusion.5
  134.0 4.8 %collective-permute-start.9 = (bf16[48,1024]{1,0:T(8,128)(2,1)S(1)}, bf16[48,1024]{1,0:T(8,128)(2,1)S(1)}, u32[]{:S(2)}, u32[]{:S(2)}) collective-permute-start(bf16[48,1024]{1,0:T(8,128)(2,1)S(1)} %convolution_convert_fusion.11), channel_id=1, source_target_pairs={{2,4},{4,2},{3,5},{5,3},{6,8},{8,6},{7,9},{9,7},{10,12},{12,10},{1... | collective-permute-start | bytes 294920 | tf_op jit(solution)/shard_map/ppermute | solution.py:44
  139.1 1.9 collective-permute-start.8
  141.1 2.7 %collective-permute-done.9 = bf16[48,1024]{1,0:T(8,128)(2,1)S(1)} collective-permute-done((bf16[48,1024]{1,0:T(8,128)(2,1)S(1)}, bf16[48,1024]{1,0:T(8,128)(2,1)S(1)}, u32[]{:S(2)}, u32[]{:S(2)}) %collective-permute-start.9) | collective-permute-done | bytes 98336 | tf_op jit(solution)/shard_map/ppermute | solution.py:44
  144.1 1.5 collective-permute-done.8
  146.0 2.4 maximum_convert_fusion.4
  149.2 4.3 %collective-permute-start.11 = (bf16[48,1024]{1,0:T(8,128)(2,1)S(1)}, bf16[48,1024]{1,0:T(8,128)(2,1)S(1)}, u32[]{:S(2)}, u32[]{:S(2)}) collective-permute-start(bf16[48,1024]{1,0:T(8,128)(2,1)S(1)} %convolution_convert_fusion.9), channel_id=1, source_target_pairs={{2,4},{4,2},{3,5},{5,3},{6,8},{8,6},{7,9},{9,7},{10,12},{12,10},{1... | collective-permute-start | bytes 294920 | tf_op jit(solution)/shard_map/ppermute | solution.py:44
  153.8 1.9 collective-permute-start.10
  155.8 3.2 %collective-permute-done.11 = bf16[48,1024]{1,0:T(8,128)(2,1)S(1)} collective-permute-done((bf16[48,1024]{1,0:T(8,128)(2,1)S(1)}, bf16[48,1024]{1,0:T(8,128)(2,1)S(1)}, u32[]{:S(2)}, u32[]{:S(2)}) %collective-permute-start.11) | collective-permute-done | bytes 98336 | tf_op jit(solution)/shard_map/ppermute | solution.py:44
  159.3 1.0 collective-permute-done.10
  160.7 2.4 maximum_convert_fusion.3
  163.9 4.8 %collective-permute-start.13 = (bf16[48,1024]{1,0:T(8,128)(2,1)S(1)}, bf16[48,1024]{1,0:T(8,128)(2,1)S(1)}, u32[]{:S(2)}, u32[]{:S(2)}) collective-permute-start(bf16[48,1024]{1,0:T(8,128)(2,1)S(1)} %convolution_convert_fusion.7), channel_id=1, source_target_pairs={{2,4},{4,2},{3,5},{5,3},{6,8},{8,6},{7,9},{9,7},{10,12},{12,10},{1... | collective-permute-start | bytes 294920 | tf_op jit(solution)/shard_map/ppermute | solution.py:44
  169.1 1.9 collective-permute-start.12
  171.0 2.7 %collective-permute-done.13 = bf16[48,1024]{1,0:T(8,128)(2,1)S(1)} collective-permute-done((bf16[48,1024]{1,0:T(8,128)(2,1)S(1)}, bf16[48,1024]{1,0:T(8,128)(2,1)S(1)}, u32[]{:S(2)}, u32[]{:S(2)}) %collective-permute-start.13) | collective-permute-done | bytes 98336 | tf_op jit(solution)/shard_map/ppermute | solution.py:44
  174.1 1.5 collective-permute-done.12
  175.9 2.4 maximum_convert_fusion.2
  179.1 4.3 %collective-permute-start.15 = (bf16[48,1024]{1,0:T(8,128)(2,1)S(1)}, bf16[48,1024]{1,0:T(8,128)(2,1)S(1)}, u32[]{:S(2)}, u32[]{:S(2)}) collective-permute-start(bf16[48,1024]{1,0:T(8,128)(2,1)S(1)} %convolution_convert_fusion.5), channel_id=1, source_target_pairs={{2,4},{4,2},{3,5},{5,3},{6,8},{8,6},{7,9},{9,7},{10,12},{12,10},{1... | collective-permute-start | bytes 294920 | tf_op jit(solution)/shard_map/ppermute | solution.py:44
  183.8 2.1 collective-permute-start.14
  185.9 3.0 %collective-permute-done.15 = bf16[48,1024]{1,0:T(8,128)(2,1)S(1)} collective-permute-done((bf16[48,1024]{1,0:T(8,128)(2,1)S(1)}, bf16[48,1024]{1,0:T(8,128)(2,1)S(1)}, u32[]{:S(2)}, u32[]{:S(2)}) %collective-permute-start.15) | collective-permute-done | bytes 98336 | tf_op jit(solution)/shard_map/ppermute | solution.py:44
  189.3 1.0 collective-permute-done.14
  190.7 2.4 maximum_convert_fusion.1
  193.8 4.8 %collective-permute-start.17 = (bf16[48,1024]{1,0:T(8,128)(2,1)S(1)}, bf16[48,1024]{1,0:T(8,128)(2,1)S(1)}, u32[]{:S(2)}, u32[]{:S(2)}) collective-permute-start(bf16[48,1024]{1,0:T(8,128)(2,1)S(1)} %convolution_convert_fusion.3), channel_id=1, source_target_pairs={{2,4},{4,2},{3,5},{5,3},{6,8},{8,6},{7,9},{9,7},{10,12},{12,10},{1... | collective-permute-start | bytes 294920 | tf_op jit(solution)/shard_map/ppermute | solution.py:44
  199.0 1.9 collective-permute-start.16
  201.0 2.7 %collective-permute-done.17 = bf16[48,1024]{1,0:T(8,128)(2,1)S(1)} collective-permute-done((bf16[48,1024]{1,0:T(8,128)(2,1)S(1)}, bf16[48,1024]{1,0:T(8,128)(2,1)S(1)}, u32[]{:S(2)}, u32[]{:S(2)}) %collective-permute-start.17) | collective-permute-done | bytes 98336 | tf_op jit(solution)/shard_map/ppermute | solution.py:44
  204.0 1.5 collective-permute-done.16
  205.9 2.4 maximum_convert_fusion
  209.1 4.3 %collective-permute-start.19 = (bf16[48,1024]{1,0:T(8,128)(2,1)S(1)}, bf16[48,1024]{1,0:T(8,128)(2,1)S(1)}, u32[]{:S(2)}, u32[]{:S(2)}) collective-permute-start(bf16[48,1024]{1,0:T(8,128)(2,1)S(1)} %convolution_convert_fusion.1), channel_id=1, source_target_pairs={{2,4},{4,2},{3,5},{5,3},{6,8},{8,6},{7,9},{9,7},{10,12},{12,10},{1... | collective-permute-start | bytes 294920 | tf_op jit(solution)/shard_map/ppermute | solution.py:44
  213.7 1.9 collective-permute-start.18
  215.7 3.2 %collective-permute-done.19 = bf16[48,1024]{1,0:T(8,128)(2,1)S(1)} collective-permute-done((bf16[48,1024]{1,0:T(8,128)(2,1)S(1)}, bf16[48,1024]{1,0:T(8,128)(2,1)S(1)}, u32[]{:S(2)}, u32[]{:S(2)}) %collective-permute-start.19) | collective-permute-done | bytes 98336 | tf_op jit(solution)/shard_map/ppermute | solution.py:44
  219.2 1.0 collective-permute-done.18
  220.6 2.3 fusion
  223.0 21.4 %all_to_all.5 = bf16[4,2,128,1024]{3,2,1,0:T(8,128)(2,1)S(1)} all-to-all(bf16[4,2,128,1024]{3,2,1,0:T(8,128)(2,1)S(1)} %bitcast.146), channel_id=1, replica_groups=mesh['segment'=4,'graph'=128] {'segment'}, dimensions={0} | all-to-all | bytes 4194304 | tf_op jit(solution)/shard_map/all_to_all | solution.py:134
  244.4 1.5 copy.28
  (107 shorter events, 23.9 us)
Async XLA Ops:
  6.5 12.2 %copy-start = (bf16[8,64,1024]{2,1,0:T(8,128)(2,1)S(1)}, bf16[8,64,1024]{2,1,0:T(8,128)(2,1)}, u32[]{:S(2)}) copy-start(bf16[8,64,1024]{2,1,0:T(8,128)(2,1)} %param.10) | copy-start | bytes 3145732
  6.5 108.8 %all-gather.2.cloned.1.call-start = ((), (), s32[]{:S(2)}) async-start(), calls=%async_computation.1 | async-start | bytes 16908288 | tf_op jit(solution)/shard_map/all_gather | solution.py:34
  8.8 12.9 %collective-permute-start.1 = (s32[128]{0:T(128)S(1)}, s32[128]{0:T(128)S(1)}, u32[]{:S(2)}, u32[]{:S(2)}) collective-permute-start(s32[128]{0:T(128)S(1)} %pad_add_fusion.4), channel_id=1, source_target_pairs={{0,1},{1,0},{2,3},{3,2},{4,5},{5,4},{6,7},{7,6},{8,9},{9,8},{10,11... | collective-permute-start | bytes 1544 | tf_op jit(solution)/shard_map/ppermute | solution.py:37
  11.7 12.1 %collective-permute-start.2 = (bf16[128,1024]{1,0:T(8,128)(2,1)S(1)}, bf16[128,1024]{1,0:T(8,128)(2,1)S(1)}, u32[]{:S(2)}, u32[]{:S(2)}) collective-permute-start(bf16[128,1024]{1,0:T(8,128)(2,1)S(1)} %constant_dynamic-slice_fusion), channel_id=1, source_target_pairs={{0,1},{1,0},{2,3},{3,2},{4,5},{5,4},{6,7},{7,6},{8,9},{9,8},{10,11... | collective-permute-start | bytes 786440 | tf_op jit(solution)/shard_map/ppermute | solution.py:37
  16.8 5.5 %collective-permute-start = (bf16[256,128]{0,1:T(8,128)(2,1)S(1)}, bf16[256,128]{0,1:T(8,128)(2,1)S(1)}, u32[]{:S(2)}, u32[]{:S(2)}) collective-permute-start(bf16[256,128]{0,1:T(8,128)(2,1)S(1)} %pad_maximum_fusion.2), channel_id=1, source_target_pairs={{0,1},{1,0},{2,3},{3,2},{4,5},{5,4},{6,7},{7,6},{8,9},{9,8},{10,11... | collective-permute-start | bytes 196616 | tf_op jit(solution)/shard_map/ppermute | solution.py:37
  19.2 16.9 %copy-start.2 = (bf16[8,64,1024]{2,1,0:T(8,128)(2,1)}, bf16[8,64,1024]{2,1,0:T(8,128)(2,1)S(1)}, u32[]{:S(2)}) copy-start(bf16[8,64,1024]{2,1,0:T(8,128)(2,1)S(1)} %fusion.8) | copy-start | bytes 3145732
  19.2 24.1 %collective-permute-start.3 = (bf16[8,64,1024]{2,1,0:T(8,128)(2,1)S(1)}, bf16[8,64,1024]{2,1,0:T(8,128)(2,1)}, u32[]{:S(2)}, u32[]{:S(2)}) collective-permute-start(bf16[8,64,1024]{2,1,0:T(8,128)(2,1)S(1)} %fusion.8), channel_id=1, source_target_pairs={{0,1},{1,0},{2,3},{3,2},{4,5},{5,4},{6,7},{7,6},{8,9},{9,8},{10,11... | collective-permute-start | bytes 3145736 | tf_op jit(solution)/shard_map/ppermute | solution.py:37
  25.1 14.0 %collective-permute-start.5 = (bf16[48,1024]{1,0:T(8,128)(2,1)S(1)}, bf16[48,1024]{1,0:T(8,128)(2,1)S(1)}, u32[]{:S(2)}, u32[]{:S(2)}) collective-permute-start(bf16[48,1024]{1,0:T(8,128)(2,1)S(1)} %convolution_convert_fusion.15), channel_id=1, source_target_pairs={{2,4},{4,2},{3,5},{5,3},{6,8},{8,6},{7,9},{9,7},{10,12},{12,10},{1... | collective-permute-start | bytes 294920 | tf_op jit(solution)/shard_map/ppermute | solution.py:44
  36.1 6.9 %collective-permute-start.4 = (bf16[48,1024]{1,0:T(8,128)(2,1)S(1)}, bf16[48,1024]{1,0:T(8,128)(2,1)S(1)}, u32[]{:S(2)}, u32[]{:S(2)}) collective-permute-start(bf16[48,1024]{1,0:T(8,128)(2,1)S(1)} %convolution_convert_fusion.16), channel_id=1, source_target_pairs={{0,2},{2,0},{1,3},{3,1},{4,6},{6,4},{5,7},{7,5},{8,10},{10,8},{9,1... | collective-permute-start | bytes 294920 | tf_op jit(solution)/shard_map/ppermute | solution.py:44
  38.1 5.3 %copy-start.3 = (bf16[8,64,1024]{2,1,0:T(8,128)(2,1)S(1)}, bf16[8,64,1024]{2,1,0:T(8,128)(2,1)}, u32[]{:S(2)}) copy-start(bf16[8,64,1024]{2,1,0:T(8,128)(2,1)} %copy-done.2) | copy-start | bytes 3145732
  119.2 10.2 %collective-permute-start.7 = (bf16[48,1024]{1,0:T(8,128)(2,1)S(1)}, bf16[48,1024]{1,0:T(8,128)(2,1)S(1)}, u32[]{:S(2)}, u32[]{:S(2)}) collective-permute-start(bf16[48,1024]{1,0:T(8,128)(2,1)S(1)} %convolution_convert_fusion.13), channel_id=1, source_target_pairs={{2,4},{4,2},{3,5},{5,3},{6,8},{8,6},{7,9},{9,7},{10,12},{12,10},{1... | collective-permute-start | bytes 294920 | tf_op jit(solution)/shard_map/ppermute | solution.py:44
  123.9 6.5 %collective-permute-start.6 = (bf16[48,1024]{1,0:T(8,128)(2,1)S(1)}, bf16[48,1024]{1,0:T(8,128)(2,1)S(1)}, u32[]{:S(2)}, u32[]{:S(2)}) collective-permute-start(bf16[48,1024]{1,0:T(8,128)(2,1)S(1)} %convolution_convert_fusion.14), channel_id=1, source_target_pairs={{0,2},{2,0},{1,3},{3,1},{4,6},{6,4},{5,7},{7,5},{8,10},{10,8},{9,1... | collective-permute-start | bytes 294920 | tf_op jit(solution)/shard_map/ppermute | solution.py:44
  134.0 9.8 %collective-permute-start.9 = (bf16[48,1024]{1,0:T(8,128)(2,1)S(1)}, bf16[48,1024]{1,0:T(8,128)(2,1)S(1)}, u32[]{:S(2)}, u32[]{:S(2)}) collective-permute-start(bf16[48,1024]{1,0:T(8,128)(2,1)S(1)} %convolution_convert_fusion.11), channel_id=1, source_target_pairs={{2,4},{4,2},{3,5},{5,3},{6,8},{8,6},{7,9},{9,7},{10,12},{12,10},{1... | collective-permute-start | bytes 294920 | tf_op jit(solution)/shard_map/ppermute | solution.py:44
  139.1 6.5 %collective-permute-start.8 = (bf16[48,1024]{1,0:T(8,128)(2,1)S(1)}, bf16[48,1024]{1,0:T(8,128)(2,1)S(1)}, u32[]{:S(2)}, u32[]{:S(2)}) collective-permute-start(bf16[48,1024]{1,0:T(8,128)(2,1)S(1)} %convolution_convert_fusion.12), channel_id=1, source_target_pairs={{0,2},{2,0},{1,3},{3,1},{4,6},{6,4},{5,7},{7,5},{8,10},{10,8},{9,1... | collective-permute-start | bytes 294920 | tf_op jit(solution)/shard_map/ppermute | solution.py:44
  149.2 9.8 %collective-permute-start.11 = (bf16[48,1024]{1,0:T(8,128)(2,1)S(1)}, bf16[48,1024]{1,0:T(8,128)(2,1)S(1)}, u32[]{:S(2)}, u32[]{:S(2)}) collective-permute-start(bf16[48,1024]{1,0:T(8,128)(2,1)S(1)} %convolution_convert_fusion.9), channel_id=1, source_target_pairs={{2,4},{4,2},{3,5},{5,3},{6,8},{8,6},{7,9},{9,7},{10,12},{12,10},{1... | collective-permute-start | bytes 294920 | tf_op jit(solution)/shard_map/ppermute | solution.py:44
  153.8 6.5 %collective-permute-start.10 = (bf16[48,1024]{1,0:T(8,128)(2,1)S(1)}, bf16[48,1024]{1,0:T(8,128)(2,1)S(1)}, u32[]{:S(2)}, u32[]{:S(2)}) collective-permute-start(bf16[48,1024]{1,0:T(8,128)(2,1)S(1)} %convolution_convert_fusion.10), channel_id=1, source_target_pairs={{0,2},{2,0},{1,3},{3,1},{4,6},{6,4},{5,7},{7,5},{8,10},{10,8},{9,1... | collective-permute-start | bytes 294920 | tf_op jit(solution)/shard_map/ppermute | solution.py:44
  163.9 9.8 %collective-permute-start.13 = (bf16[48,1024]{1,0:T(8,128)(2,1)S(1)}, bf16[48,1024]{1,0:T(8,128)(2,1)S(1)}, u32[]{:S(2)}, u32[]{:S(2)}) collective-permute-start(bf16[48,1024]{1,0:T(8,128)(2,1)S(1)} %convolution_convert_fusion.7), channel_id=1, source_target_pairs={{2,4},{4,2},{3,5},{5,3},{6,8},{8,6},{7,9},{9,7},{10,12},{12,10},{1... | collective-permute-start | bytes 294920 | tf_op jit(solution)/shard_map/ppermute | solution.py:44
  169.1 6.5 %collective-permute-start.12 = (bf16[48,1024]{1,0:T(8,128)(2,1)S(1)}, bf16[48,1024]{1,0:T(8,128)(2,1)S(1)}, u32[]{:S(2)}, u32[]{:S(2)}) collective-permute-start(bf16[48,1024]{1,0:T(8,128)(2,1)S(1)} %convolution_convert_fusion.8), channel_id=1, source_target_pairs={{0,2},{2,0},{1,3},{3,1},{4,6},{6,4},{5,7},{7,5},{8,10},{10,8},{9,1... | collective-permute-start | bytes 294920 | tf_op jit(solution)/shard_map/ppermute | solution.py:44
  179.1 9.8 %collective-permute-start.15 = (bf16[48,1024]{1,0:T(8,128)(2,1)S(1)}, bf16[48,1024]{1,0:T(8,128)(2,1)S(1)}, u32[]{:S(2)}, u32[]{:S(2)}) collective-permute-start(bf16[48,1024]{1,0:T(8,128)(2,1)S(1)} %convolution_convert_fusion.5), channel_id=1, source_target_pairs={{2,4},{4,2},{3,5},{5,3},{6,8},{8,6},{7,9},{9,7},{10,12},{12,10},{1... | collective-permute-start | bytes 294920 | tf_op jit(solution)/shard_map/ppermute | solution.py:44
  183.8 6.5 %collective-permute-start.14 = (bf16[48,1024]{1,0:T(8,128)(2,1)S(1)}, bf16[48,1024]{1,0:T(8,128)(2,1)S(1)}, u32[]{:S(2)}, u32[]{:S(2)}) collective-permute-start(bf16[48,1024]{1,0:T(8,128)(2,1)S(1)} %convolution_convert_fusion.6), channel_id=1, source_target_pairs={{0,2},{2,0},{1,3},{3,1},{4,6},{6,4},{5,7},{7,5},{8,10},{10,8},{9,1... | collective-permute-start | bytes 294920 | tf_op jit(solution)/shard_map/ppermute | solution.py:44
  193.8 9.8 %collective-permute-start.17 = (bf16[48,1024]{1,0:T(8,128)(2,1)S(1)}, bf16[48,1024]{1,0:T(8,128)(2,1)S(1)}, u32[]{:S(2)}, u32[]{:S(2)}) collective-permute-start(bf16[48,1024]{1,0:T(8,128)(2,1)S(1)} %convolution_convert_fusion.3), channel_id=1, source_target_pairs={{2,4},{4,2},{3,5},{5,3},{6,8},{8,6},{7,9},{9,7},{10,12},{12,10},{1... | collective-permute-start | bytes 294920 | tf_op jit(solution)/shard_map/ppermute | solution.py:44
  199.0 6.5 %collective-permute-start.16 = (bf16[48,1024]{1,0:T(8,128)(2,1)S(1)}, bf16[48,1024]{1,0:T(8,128)(2,1)S(1)}, u32[]{:S(2)}, u32[]{:S(2)}) collective-permute-start(bf16[48,1024]{1,0:T(8,128)(2,1)S(1)} %convolution_convert_fusion.4), channel_id=1, source_target_pairs={{0,2},{2,0},{1,3},{3,1},{4,6},{6,4},{5,7},{7,5},{8,10},{10,8},{9,1... | collective-permute-start | bytes 294920 | tf_op jit(solution)/shard_map/ppermute | solution.py:44
  209.1 9.8 %collective-permute-start.19 = (bf16[48,1024]{1,0:T(8,128)(2,1)S(1)}, bf16[48,1024]{1,0:T(8,128)(2,1)S(1)}, u32[]{:S(2)}, u32[]{:S(2)}) collective-permute-start(bf16[48,1024]{1,0:T(8,128)(2,1)S(1)} %convolution_convert_fusion.1), channel_id=1, source_target_pairs={{2,4},{4,2},{3,5},{5,3},{6,8},{8,6},{7,9},{9,7},{10,12},{12,10},{1... | collective-permute-start | bytes 294920 | tf_op jit(solution)/shard_map/ppermute | solution.py:44
  213.7 6.5 %collective-permute-start.18 = (bf16[48,1024]{1,0:T(8,128)(2,1)S(1)}, bf16[48,1024]{1,0:T(8,128)(2,1)S(1)}, u32[]{:S(2)}, u32[]{:S(2)}) collective-permute-start(bf16[48,1024]{1,0:T(8,128)(2,1)S(1)} %convolution_convert_fusion.2), channel_id=1, source_target_pairs={{0,2},{2,0},{1,3},{3,1},{4,6},{6,4},{5,7},{7,5},{8,10},{10,8},{9,1... | collective-permute-start | bytes 294920 | tf_op jit(solution)/shard_map/ppermute | solution.py:44
  244.4 1.5 copy-start.1
Sparse Core Ops, SparseCore 0:
  10.6 104.6 all-gather.1
where the time goes:
time: 254 us; the launch traced here: 253 us
  waiting for transfers between devices  104 us (41%)
  starting transfers between devices  66.9 us (26%)
  matrix products  35.9 us (14%)
  blocking collectives  21.4 us (8%)
  between operations  14.1 us (6%)
  local copies, waits for them, and re-layouts  7.57 us (3%)
  other arithmetic  3.38 us (1%)
    all_gather x1, waiting for transfers between devices, shards(): resident = lax.all_gather(weights, 'graph', axis=1, tiled=True)  68.9 us
    ppermute x16, starting transfers between devices, exchange(): return lax.ppermute(value, 'graph', pairs)  58.2 us
    ppermute x16, waiting for transfers between devices, exchange(): return lax.ppermute(value, 'graph', pairs)  34 us
    dot_general x33, matrix products, dot(): return jnp.dot(a, b, preferred_element_type=F32)  27.5 us
    all_to_all x1, blocking collectives, shards(): exchanged = lax.all_to_all(whole, 'segment', 0, 0)  21.4 us
    ppermute x4, starting transfers between devices, partner(): lax.ppermute(value, 'graph', [(p, p ^ 1) for p in range(graph_count)])  8.64 us
    dot_general x26, matrix products, dot_t(): lax.dot_general(a, b, (((0,), (0,)), ((), ())), preferred_element_type=F32)  8.4 us
  transfers between devices with their start and end apart: 21, of which 17 were waited for; matrix products, arithmetic and copies ran while one was open for 7% of the time, Pallas kernels for 0%

commit v1 on v0

--- a/solution.py
+++ b/solution.py
@@ -31,7 +31,9 @@
     rows = own_adj.shape[2]
     edge = send_ids.shape[2]
     kept = layers // segment_count
-    resident = lax.all_gather(weights, "graph", axis=1, tiled=True)
+    resident = jnp.concatenate(
+        lax.all_to_all(jnp.stack([weights] * lax.axis_size("graph")), "graph", 0, 0), axis=1
+    )
 
     def partner(value):
         return lax.ppermute(value, "graph", [(p, p ^ 1) for p in range(graph_count)])

time: 254 us -> 690 us (2.72)
  waiting for transfers between devices: 104 us -> 513 us
  starting transfers between devices: 66.9 us -> 99.4 us
  between operations: 14.1 us -> 0.8 us
    ppermute x16, waiting for transfers between devices: 34 us -> 344 us  [exchange(): return lax.ppermute(value, 'graph', pairs)]
    all_to_all x0 -> x1, waiting for transfers between devices: none -> 169 us  [shards(): lax.all_to_all(jnp.stack([weights] * lax.axis_size('graph')), 'graph', 0, 0)]
    all_gather x1 -> x0, waiting for transfers between devices: 68.9 us -> none  [shards(): resident = lax.all_gather(weights, 'graph', axis=1, tiled=True)]
    all_to_all x0 -> x1, starting transfers between devices: none -> 17.9 us  [shards(): lax.all_to_all(jnp.stack([weights] * lax.axis_size('graph')), 'graph', 0, 0)]
    ppermute x16, starting transfers between devices: 58.2 us -> 72.9 us  [exchange(): return lax.ppermute(value, 'graph', pairs)]
  transfers between devices with their start and end apart: 21 -> 21, of which waited for: 17 -> 10; matrix products, arithmetic and copies ran while one was open for 7% -> 3% of each run, Pallas kernels for 0% -> 0%
where the time goes in v1:
time: 690 us; the launch traced here: 689 us
  waiting for transfers between devices  513 us (74%)
  starting transfers between devices  99.4 us (14%)
  matrix products  35.9 us (5%)
  blocking collectives  22.3 us (3%)
  local copies, waits for them, and re-layouts  14.2 us (2%)
    ppermute x16, waiting for transfers between devices, exchange(): return lax.ppermute(value, 'graph', pairs)  344 us
    all_to_all x1, waiting for transfers between devices, shards(): lax.all_to_all(jnp.stack([weights] * lax.axis_size('graph')), 'graph', 0, 0)  169 us
    ppermute x16, starting transfers between devices, exchange(): return lax.ppermute(value, 'graph', pairs)  72.9 us
    dot_general x33, matrix products, dot(): return jnp.dot(a, b, preferred_element_type=F32)  27.4 us
    all_to_all x1, blocking collectives, shards(): exchanged = lax.all_to_all(whole, 'segment', 0, 0)  22.3 us
    all_to_all x1, starting transfers between devices, shards(): lax.all_to_all(jnp.stack([weights] * lax.axis_size('graph')), 'graph', 0, 0)  17.9 us
  transfers between devices with their start and end apart: 21, of which 10 were waited for; matrix products, arithmetic and copies ran while one was open for 3% of the time, Pallas kernels for 0%

profile of v1, /device:TPU:32, one launch (start us, length us, event | category | flops | bytes accessed | tf_op | source)
XLA Modules:
  0.0 689.0 jit_solution(9694991521052842440)
XLA Ops:
  0.0 6.9 stack.20
  6.9 17.9 %all-to-all-start = ((bf16[128,8,8,1024]{3,2,1,0:T(8,128)(2,1)}), bf16[128,8,8,1024]{3,2,1,0:T(8,128)(2,1)}, u32[]{:S(2)}, u32[]{:S(2)}) async-start(bf16[128,8,8,1024]{3,2,1,0:T(8,128)(2,1)} %stack.20), calls=%async_computation | async-start | bytes 33554432 | tf_op jit(solution)/shard_map/all_to_all | solution.py:35
  26.4 2.0 collective-permute-start.1
  29.2 0.7 constant_dynamic-slice_fusion.3
  30.1 0.8 constant_dynamic-slice_fusion.5
  31.7 2.3 collective-permute-start
  34.0 0.7 constant_dynamic-slice_fusion
  34.7 2.0 collective-permute-start.2
  37.2 2.3 collective-permute-start.3
  40.2 0.9 broadcast_select_fusion.5
  42.9 3.4 collective-permute-start.4
  46.5 4.5 collective-permute-start.5
  51.0 284.1 %collective-permute-done.4 = bf16[48,1024]{1,0:T(8,128)(2,1)S(1)} collective-permute-done((bf16[48,1024]{1,0:T(8,128)(2,1)S(1)}, bf16[48,1024]{1,0:T(8,128)(2,1)S(1)}, u32[]{:S(2)}, u32[]{:S(2)}) %collective-permute-start.4) | collective-permute-done | bytes 98336 | tf_op jit(solution)/shard_map/ppermute | solution.py:46
  335.4 7.8 %collective-permute-done.5 = bf16[48,1024]{1,0:T(8,128)(2,1)S(1)} collective-permute-done((bf16[48,1024]{1,0:T(8,128)(2,1)S(1)}, bf16[48,1024]{1,0:T(8,128)(2,1)S(1)}, u32[]{:S(2)}, u32[]{:S(2)}) %collective-permute-start.5) | collective-permute-done | bytes 98336 | tf_op jit(solution)/shard_map/ppermute | solution.py:46
  343.5 1.4 broadcast_select_fusion
  345.2 1.4 fusion.19
  346.6 168.8 %all-to-all-done = bf16[128,8,8,1024]{3,2,1,0:T(8,128)(2,1)} async-done(((bf16[128,8,8,1024]{3,2,1,0:T(8,128)(2,1)}), bf16[128,8,8,1024]{3,2,1,0:T(8,128)(2,1)}, u32[]{:S(2)}, u32[]{:S(2)}) %all-to-all-start) | async-done | bytes 16777248 | tf_op jit(solution)/shard_map/all_to_all | solution.py:35
  515.5 3.0 maximum_convert_fusion.6
  519.3 38.9 %collective-permute-start.6 = (bf16[48,1024]{1,0:T(8,128)(2,1)S(1)}, bf16[48,1024]{1,0:T(8,128)(2,1)S(1)}, u32[]{:S(2)}, u32[]{:S(2)}) collective-permute-start(bf16[48,1024]{1,0:T(8,128)(2,1)S(1)} %convolution_convert_fusion.14), channel_id=1, source_target_pairs={{0,2},{2,0},{1,3},{3,1},{4,6},{6,4},{5,7},{7,5},{8,10},{10,8},{9,1... | collective-permute-start | bytes 294920 | tf_op jit(solution)/shard_map/ppermute | solution.py:46
  558.2 1.9 collective-permute-start.7
  560.5 7.6 %collective-permute-done.7 = bf16[48,1024]{1,0:T(8,128)(2,1)S(1)} collective-permute-done((bf16[48,1024]{1,0:T(8,128)(2,1)S(1)}, bf16[48,1024]{1,0:T(8,128)(2,1)S(1)}, u32[]{:S(2)}, u32[]{:S(2)}) %collective-permute-start.7) | collective-permute-done | bytes 98336 | tf_op jit(solution)/shard_map/ppermute | solution.py:46
  568.8 2.4 maximum_convert_fusion.5
  571.9 1.9 collective-permute-start.8
  573.9 2.1 collective-permute-start.9
  576.3 7.4 %collective-permute-done.9 = bf16[48,1024]{1,0:T(8,128)(2,1)S(1)} collective-permute-done((bf16[48,1024]{1,0:T(8,128)(2,1)S(1)}, bf16[48,1024]{1,0:T(8,128)(2,1)S(1)}, u32[]{:S(2)}, u32[]{:S(2)}) %collective-permute-start.9) | collective-permute-done | bytes 98336 | tf_op jit(solution)/shard_map/ppermute | solution.py:46
  584.4 2.4 maximum_convert_fusion.4
  587.6 1.9 collective-permute-start.10
  589.5 2.1 collective-permute-start.11
  591.9 7.4 %collective-permute-done.11 = bf16[48,1024]{1,0:T(8,128)(2,1)S(1)} collective-permute-done((bf16[48,1024]{1,0:T(8,128)(2,1)S(1)}, bf16[48,1024]{1,0:T(8,128)(2,1)S(1)}, u32[]{:S(2)}, u32[]{:S(2)}) %collective-permute-start.11) | collective-permute-done | bytes 98336 | tf_op jit(solution)/shard_map/ppermute | solution.py:46
  600.1 2.4 maximum_convert_fusion.3
  603.3 1.9 collective-permute-start.12
  605.2 2.2 collective-permute-start.13
  607.8 7.2 %collective-permute-done.13 = bf16[48,1024]{1,0:T(8,128)(2,1)S(1)} collective-permute-done((bf16[48,1024]{1,0:T(8,128)(2,1)S(1)}, bf16[48,1024]{1,0:T(8,128)(2,1)S(1)}, u32[]{:S(2)}, u32[]{:S(2)}) %collective-permute-start.13) | collective-permute-done | bytes 98336 | tf_op jit(solution)/shard_map/ppermute | solution.py:46
  615.7 2.4 maximum_convert_fusion.2
  618.9 1.9 collective-permute-start.14
  620.9 2.1 collective-permute-start.15
  623.3 7.4 %collective-permute-done.15 = bf16[48,1024]{1,0:T(8,128)(2,1)S(1)} collective-permute-done((bf16[48,1024]{1,0:T(8,128)(2,1)S(1)}, bf16[48,1024]{1,0:T(8,128)(2,1)S(1)}, u32[]{:S(2)}, u32[]{:S(2)}) %collective-permute-start.15) | collective-permute-done | bytes 98336 | tf_op jit(solution)/shard_map/ppermute | solution.py:46
  631.4 2.4 maximum_convert_fusion.1
  634.6 1.9 collective-permute-start.16
  636.5 2.1 collective-permute-start.17
  638.9 7.4 %collective-permute-done.17 = bf16[48,1024]{1,0:T(8,128)(2,1)S(1)} collective-permute-done((bf16[48,1024]{1,0:T(8,128)(2,1)S(1)}, bf16[48,1024]{1,0:T(8,128)(2,1)S(1)}, u32[]{:S(2)}, u32[]{:S(2)}) %collective-permute-start.17) | collective-permute-done | bytes 98336 | tf_op jit(solution)/shard_map/ppermute | solution.py:46
  647.1 2.4 maximum_convert_fusion
  650.3 1.9 collective-permute-start.18
  652.2 2.1 collective-permute-start.19
  654.6 7.4 %collective-permute-done.19 = bf16[48,1024]{1,0:T(8,128)(2,1)S(1)} collective-permute-done((bf16[48,1024]{1,0:T(8,128)(2,1)S(1)}, bf16[48,1024]{1,0:T(8,128)(2,1)S(1)}, u32[]{:S(2)}, u32[]{:S(2)}) %collective-permute-start.19) | collective-permute-done | bytes 98336 | tf_op jit(solution)/shard_map/ppermute | solution.py:46
  662.7 2.3 fusion
  665.2 22.3 %all_to_all.10 = bf16[4,2,128,1024]{3,2,1,0:T(8,128)(2,1)S(1)} all-to-all(bf16[4,2,128,1024]{3,2,1,0:T(8,128)(2,1)S(1)} %bitcast.147), channel_id=1, replica_groups=mesh['segment'=4,'graph'=128] {'segment'}, dimensions={0} | all-to-all | bytes 4194304 | tf_op jit(solution)/shard_map/all_to_all | solution.py:136
  687.5 1.5 copy.28
  (109 shorter events, 19.8 us)
Async XLA Ops:
  0.0 36.7 %copy-start = (bf16[8,64,1024]{2,1,0:T(8,128)(2,1)S(1)}, bf16[8,64,1024]{2,1,0:T(8,128)(2,1)}, u32[]{:S(2)}) copy-start(bf16[8,64,1024]{2,1,0:T(8,128)(2,1)} %param.10) | copy-start | bytes 3145732
  6.9 27.1 %copy-start.4 = (bf16[512,1024]{1,0:T(8,128)(2,1)S(1)}, bf16[512,1024]{1,0:T(8,128)(2,1)}, u32[]{:S(2)}) copy-start(bf16[512,1024]{1,0:T(8,128)(2,1)} %param.8) | copy-start | bytes 3145732
  6.9 508.6 %all-to-all-start = ((bf16[128,8,8,1024]{3,2,1,0:T(8,128)(2,1)}), bf16[128,8,8,1024]{3,2,1,0:T(8,128)(2,1)}, u32[]{:S(2)}, u32[]{:S(2)}) async-start(bf16[128,8,8,1024]{3,2,1,0:T(8,128)(2,1)} %stack.20), calls=%async_computation | async-start | bytes 33554432 | tf_op jit(solution)/shard_map/all_to_all | solution.py:35
  26.4 13.2 %collective-permute-start.1 = (s32[128]{0:T(128)S(1)}, s32[128]{0:T(128)S(1)}, u32[]{:S(2)}, u32[]{:S(2)}) collective-permute-start(s32[128]{0:T(128)S(1)} %pad_add_fusion.4), channel_id=1, source_target_pairs={{0,1},{1,0},{2,3},{3,2},{4,5},{5,4},{6,7},{7,6},{8,9},{9,8},{10,11... | collective-permute-start | bytes 1544 | tf_op jit(solution)/shard_map/ppermute | solution.py:39
  31.7 8.5 %collective-permute-start = (bf16[256,128]{0,1:T(8,128)(2,1)}, bf16[256,128]{0,1:T(8,128)(2,1)}, u32[]{:S(2)}, u32[]{:S(2)}) collective-permute-start(bf16[256,128]{0,1:T(8,128)(2,1)} %pad_maximum_fusion.2), channel_id=1, source_target_pairs={{0,1},{1,0},{2,3},{3,2},{4,5},{5,4},{6,7},{7,6},{8,9},{9,8},{10,11... | collective-permute-start | bytes 196616 | tf_op jit(solution)/shard_map/ppermute | solution.py:39
  34.7 7.8 %collective-permute-start.2 = (bf16[128,1024]{1,0:T(8,128)(2,1)}, bf16[128,1024]{1,0:T(8,128)(2,1)S(1)}, u32[]{:S(2)}, u32[]{:S(2)}) collective-permute-start(bf16[128,1024]{1,0:T(8,128)(2,1)} %constant_dynamic-slice_fusion), channel_id=1, source_target_pairs={{0,1},{1,0},{2,3},{3,2},{4,5},{5,4},{6,7},{7,6},{8,9},{9,8},{10,11... | collective-permute-start | bytes 786440 | tf_op jit(solution)/shard_map/ppermute | solution.py:39
  37.2 9.2 %copy-start.2 = (bf16[8,64,1024]{2,1,0:T(8,128)(2,1)}, bf16[8,64,1024]{2,1,0:T(8,128)(2,1)S(1)}, u32[]{:S(2)}) copy-start(bf16[8,64,1024]{2,1,0:T(8,128)(2,1)S(1)} %fusion.8) | copy-start | bytes 3145732
  37.2 306.3 %collective-permute-start.3 = (bf16[8,64,1024]{2,1,0:T(8,128)(2,1)S(1)}, bf16[8,64,1024]{2,1,0:T(8,128)(2,1)}, u32[]{:S(2)}, u32[]{:S(2)}) collective-permute-start(bf16[8,64,1024]{2,1,0:T(8,128)(2,1)S(1)} %fusion.8), channel_id=1, source_target_pairs={{0,1},{1,0},{2,3},{3,2},{4,5},{5,4},{6,7},{7,6},{8,9},{9,8},{10,11... | collective-permute-start | bytes 3145736 | tf_op jit(solution)/shard_map/ppermute | solution.py:39
  42.9 292.2 %collective-permute-start.4 = (bf16[48,1024]{1,0:T(8,128)(2,1)S(1)}, bf16[48,1024]{1,0:T(8,128)(2,1)S(1)}, u32[]{:S(2)}, u32[]{:S(2)}) collective-permute-start(bf16[48,1024]{1,0:T(8,128)(2,1)S(1)} %convolution_convert_fusion.16), channel_id=1, source_target_pairs={{0,2},{2,0},{1,3},{3,1},{4,6},{6,4},{5,7},{7,5},{8,10},{10,8},{9,1... | collective-permute-start | bytes 294920 | tf_op jit(solution)/shard_map/ppermute | solution.py:46
  46.5 296.7 %collective-permute-start.5 = (bf16[48,1024]{1,0:T(8,128)(2,1)S(1)}, bf16[48,1024]{1,0:T(8,128)(2,1)S(1)}, u32[]{:S(2)}, u32[]{:S(2)}) collective-permute-start(bf16[48,1024]{1,0:T(8,128)(2,1)S(1)} %convolution_convert_fusion.15), channel_id=1, source_target_pairs={{2,4},{4,2},{3,5},{5,3},{6,8},{8,6},{7,9},{9,7},{10,12},{12,10},{1... | collective-permute-start | bytes 294920 | tf_op jit(solution)/shard_map/ppermute | solution.py:46
  51.0 292.5 %copy-start.3 = (bf16[8,64,1024]{2,1,0:T(8,128)(2,1)S(1)}, bf16[8,64,1024]{2,1,0:T(8,128)(2,1)}, u32[]{:S(2)}) copy-start(bf16[8,64,1024]{2,1,0:T(8,128)(2,1)} %copy-done.2) | copy-start | bytes 3145732
  519.3 49.1 %collective-permute-start.6 = (bf16[48,1024]{1,0:T(8,128)(2,1)S(1)}, bf16[48,1024]{1,0:T(8,128)(2,1)S(1)}, u32[]{:S(2)}, u32[]{:S(2)}) collective-permute-start(bf16[48,1024]{1,0:T(8,128)(2,1)S(1)} %convolution_convert_fusion.14), channel_id=1, source_target_pairs={{0,2},{2,0},{1,3},{3,1},{4,6},{6,4},{5,7},{7,5},{8,10},{10,8},{9,1... | collective-permute-start | bytes 294920 | tf_op jit(solution)/shard_map/ppermute | solution.py:46
  558.2 9.8 %collective-permute-start.7 = (bf16[48,1024]{1,0:T(8,128)(2,1)S(1)}, bf16[48,1024]{1,0:T(8,128)(2,1)S(1)}, u32[]{:S(2)}, u32[]{:S(2)}) collective-permute-start(bf16[48,1024]{1,0:T(8,128)(2,1)S(1)} %convolution_convert_fusion.13), channel_id=1, source_target_pairs={{2,4},{4,2},{3,5},{5,3},{6,8},{8,6},{7,9},{9,7},{10,12},{12,10},{1... | collective-permute-start | bytes 294920 | tf_op jit(solution)/shard_map/ppermute | solution.py:46
  571.9 12.1 %collective-permute-start.8 = (bf16[48,1024]{1,0:T(8,128)(2,1)S(1)}, bf16[48,1024]{1,0:T(8,128)(2,1)S(1)}, u32[]{:S(2)}, u32[]{:S(2)}) collective-permute-start(bf16[48,1024]{1,0:T(8,128)(2,1)S(1)} %convolution_convert_fusion.12), channel_id=1, source_target_pairs={{0,2},{2,0},{1,3},{3,1},{4,6},{6,4},{5,7},{7,5},{8,10},{10,8},{9,1... | collective-permute-start | bytes 294920 | tf_op jit(solution)/shard_map/ppermute | solution.py:46
  573.9 9.8 %collective-permute-start.9 = (bf16[48,1024]{1,0:T(8,128)(2,1)S(1)}, bf16[48,1024]{1,0:T(8,128)(2,1)S(1)}, u32[]{:S(2)}, u32[]{:S(2)}) collective-permute-start(bf16[48,1024]{1,0:T(8,128)(2,1)S(1)} %convolution_convert_fusion.11), channel_id=1, source_target_pairs={{2,4},{4,2},{3,5},{5,3},{6,8},{8,6},{7,9},{9,7},{10,12},{12,10},{1... | collective-permute-start | bytes 294920 | tf_op jit(solution)/shard_map/ppermute | solution.py:46
  587.6 12.1 %collective-permute-start.10 = (bf16[48,1024]{1,0:T(8,128)(2,1)S(1)}, bf16[48,1024]{1,0:T(8,128)(2,1)S(1)}, u32[]{:S(2)}, u32[]{:S(2)}) collective-permute-start(bf16[48,1024]{1,0:T(8,128)(2,1)S(1)} %convolution_convert_fusion.10), channel_id=1, source_target_pairs={{0,2},{2,0},{1,3},{3,1},{4,6},{6,4},{5,7},{7,5},{8,10},{10,8},{9,1... | collective-permute-start | bytes 294920 | tf_op jit(solution)/shard_map/ppermute | solution.py:46
  589.5 9.8 %collective-permute-start.11 = (bf16[48,1024]{1,0:T(8,128)(2,1)S(1)}, bf16[48,1024]{1,0:T(8,128)(2,1)S(1)}, u32[]{:S(2)}, u32[]{:S(2)}) collective-permute-start(bf16[48,1024]{1,0:T(8,128)(2,1)S(1)} %convolution_convert_fusion.9), channel_id=1, source_target_pairs={{2,4},{4,2},{3,5},{5,3},{6,8},{8,6},{7,9},{9,7},{10,12},{12,10},{1... | collective-permute-start | bytes 294920 | tf_op jit(solution)/shard_map/ppermute | solution.py:46
  603.3 12.1 %collective-permute-start.12 = (bf16[48,1024]{1,0:T(8,128)(2,1)S(1)}, bf16[48,1024]{1,0:T(8,128)(2,1)S(1)}, u32[]{:S(2)}, u32[]{:S(2)}) collective-permute-start(bf16[48,1024]{1,0:T(8,128)(2,1)S(1)} %convolution_convert_fusion.8), channel_id=1, source_target_pairs={{0,2},{2,0},{1,3},{3,1},{4,6},{6,4},{5,7},{7,5},{8,10},{10,8},{9,1... | collective-permute-start | bytes 294920 | tf_op jit(solution)/shard_map/ppermute | solution.py:46
  605.2 9.8 %collective-permute-start.13 = (bf16[48,1024]{1,0:T(8,128)(2,1)S(1)}, bf16[48,1024]{1,0:T(8,128)(2,1)S(1)}, u32[]{:S(2)}, u32[]{:S(2)}) collective-permute-start(bf16[48,1024]{1,0:T(8,128)(2,1)S(1)} %convolution_convert_fusion.7), channel_id=1, source_target_pairs={{2,4},{4,2},{3,5},{5,3},{6,8},{8,6},{7,9},{9,7},{10,12},{12,10},{1... | collective-permute-start | bytes 294920 | tf_op jit(solution)/shard_map/ppermute | solution.py:46
  618.9 12.1 %collective-permute-start.14 = (bf16[48,1024]{1,0:T(8,128)(2,1)S(1)}, bf16[48,1024]{1,0:T(8,128)(2,1)S(1)}, u32[]{:S(2)}, u32[]{:S(2)}) collective-permute-start(bf16[48,1024]{1,0:T(8,128)(2,1)S(1)} %convolution_convert_fusion.6), channel_id=1, source_target_pairs={{0,2},{2,0},{1,3},{3,1},{4,6},{6,4},{5,7},{7,5},{8,10},{10,8},{9,1... | collective-permute-start | bytes 294920 | tf_op jit(solution)/shard_map/ppermute | solution.py:46
  620.9 9.8 %collective-permute-start.15 = (bf16[48,1024]{1,0:T(8,128)(2,1)S(1)}, bf16[48,1024]{1,0:T(8,128)(2,1)S(1)}, u32[]{:S(2)}, u32[]{:S(2)}) collective-permute-start(bf16[48,1024]{1,0:T(8,128)(2,1)S(1)} %convolution_convert_fusion.5), channel_id=1, source_target_pairs={{2,4},{4,2},{3,5},{5,3},{6,8},{8,6},{7,9},{9,7},{10,12},{12,10},{1... | collective-permute-start | bytes 294920 | tf_op jit(solution)/shard_map/ppermute | solution.py:46
  634.6 12.1 %collective-permute-start.16 = (bf16[48,1024]{1,0:T(8,128)(2,1)S(1)}, bf16[48,1024]{1,0:T(8,128)(2,1)S(1)}, u32[]{:S(2)}, u32[]{:S(2)}) collective-permute-start(bf16[48,1024]{1,0:T(8,128)(2,1)S(1)} %convolution_convert_fusion.4), channel_id=1, source_target_pairs={{0,2},{2,0},{1,3},{3,1},{4,6},{6,4},{5,7},{7,5},{8,10},{10,8},{9,1... | collective-permute-start | bytes 294920 | tf_op jit(solution)/shard_map/ppermute | solution.py:46
  636.5 9.8 %collective-permute-start.17 = (bf16[48,1024]{1,0:T(8,128)(2,1)S(1)}, bf16[48,1024]{1,0:T(8,128)(2,1)S(1)}, u32[]{:S(2)}, u32[]{:S(2)}) collective-permute-start(bf16[48,1024]{1,0:T(8,128)(2,1)S(1)} %convolution_convert_fusion.3), channel_id=1, source_target_pairs={{2,4},{4,2},{3,5},{5,3},{6,8},{8,6},{7,9},{9,7},{10,12},{12,10},{1... | collective-permute-start | bytes 294920 | tf_op jit(solution)/shard_map/ppermute | solution.py:46
  650.3 12.1 %collective-permute-start.18 = (bf16[48,1024]{1,0:T(8,128)(2,1)S(1)}, bf16[48,1024]{1,0:T(8,128)(2,1)S(1)}, u32[]{:S(2)}, u32[]{:S(2)}) collective-permute-start(bf16[48,1024]{1,0:T(8,128)(2,1)S(1)} %convolution_convert_fusion.2), channel_id=1, source_target_pairs={{0,2},{2,0},{1,3},{3,1},{4,6},{6,4},{5,7},{7,5},{8,10},{10,8},{9,1... | collective-permute-start | bytes 294920 | tf_op jit(solution)/shard_map/ppermute | solution.py:46
  652.2 9.8 %collective-permute-start.19 = (bf16[48,1024]{1,0:T(8,128)(2,1)S(1)}, bf16[48,1024]{1,0:T(8,128)(2,1)S(1)}, u32[]{:S(2)}, u32[]{:S(2)}) collective-permute-start(bf16[48,1024]{1,0:T(8,128)(2,1)S(1)} %convolution_convert_fusion.1), channel_id=1, source_target_pairs={{2,4},{4,2},{3,5},{5,3},{6,8},{8,6},{7,9},{9,7},{10,12},{12,10},{1... | collective-permute-start | bytes 294920 | tf_op jit(solution)/shard_map/ppermute | solution.py:46
  687.5 1.5 copy-start.1
